TPU v7x, 512 devices: a whole 4x4x16 slice. The times are simulated.
512 devices in a mesh: feeder: 32 (over x, y, core), scen: 16 (over z).
Axes of the slice: x: 4, y: 4, z: 16, core: 2. Of those that a mesh axis runs over, the one named last changes fastest.
Arguments:
- anchor: bfloat16 [256, 24, 16384], P('scen', None, 'feeder'), may hold values from -6 to 6
- cost_lin: bfloat16 [256, 24, 16384], P('scen', None, 'feeder'), may hold values from -6 to 6
- dual: float32 [256, 24, 16384], P('scen', None, 'feeder'), may hold values from -4 to 4
- target: float32 [256, 24], P('scen'), may hold values from -4 to 4
- leaf_weight: float32 [256], P('scen'), may hold values from 1 to 10
- q_mat: bfloat16 [16384, 512], P('feeder'), may hold values from -0.25 to 0.25
- diag_gain: float32 [16384], P('feeder'), may hold values from 0.5 to 2
- block_mask: int32 [32, 4, 4], P('feeder'), may hold values from 0 to 1, as said below
- ancestor: int32 [24, 256], P(None, 'scen'), may hold values from 0 to 255, as said below
Outputs:
- setpoints: float32 [256, 24, 16384], P('scen', None, 'feeder')
- average: float32 [256, 24, 16384], P('scen', None, 'feeder')
- new_dual: float32 [256, 24, 16384], P('scen', None, 'feeder')
Inputs may be any that keep to these rules, and one draw needn't show every extreme that they name: `block_mask`: every diagonal block is present; the share of present off-diagonal blocks differs from feeder to feeder. ancestor[t, s] is the first leaf of the section-t tree node that holds leaf s: the leaves of a node are consecutive, ancestor[0, s] = 0, and every section-t node lies inside one section-(t-1) node. Nodes may span several groups at any section.
All inputs are finite; a program needn't handle non-finite values.
Results may differ from a plain program's by a relative error of at most 0.0003.
Values sent between devices are 32-bit elements; how exact they have to be, the bound alone decides.
No kernel may reach another device: no remote copies, remote signals or barrier semaphores. Data moves between devices by JAX's collectives and lax.ppermute only.
A program may use at most 64 MiB of HBM per device.

v0:
```python
import jax
import jax.numpy as jnp
from jax import lax
from jax.sharding import PartitionSpec as P

PROX_ITERS = 8
penalty = 1.0
step_size = 0.08
coupling = 4.0
power_limit = 2.0


def link_terms(earlier, later):
    return (
        later[0] + later[2][:, None] * earlier[0],
        later[1] + later[2] * earlier[1],
        earlier[2] * later[2],
    )


def local(anchor, cost_lin, dual, target, leaf_weight, q_mat, diag_gain, block_mask, ancestor):
    leaves, sections, nodes = anchor.shape
    rows = leaves * sections
    count = block_mask.shape[1]
    width = nodes // count
    total_nodes = lax.axis_size("feeder") * nodes
    start_pt = anchor.astype(jnp.float32)
    fixed_part = cost_lin.astype(jnp.float32) + dual - penalty * start_pt
    diag_term = 2.0 * diag_gain + penalty
    expand = jnp.repeat(jnp.repeat(block_mask[0], width, axis=0), width, axis=1).astype(
        jnp.bfloat16
    )
    q_eff = q_mat * expand
    state = start_pt
    for sweep in range(PROX_ITERS):
        flat = state.reshape(rows, nodes).astype(jnp.bfloat16)
        image = jnp.dot(flat, q_eff, preferred_element_type=jnp.float32)
        head = lax.psum(jnp.sum(state, axis=2), "feeder") / total_nodes
        grad = image.reshape(leaves, sections, nodes) + diag_term * state + fixed_part
        grad = grad + coupling * (head - target)[:, :, None]
        state = jnp.clip(state - step_size * grad, -power_limit, power_limit)
    highest = lax.Precision.HIGHEST
    weighted = leaf_weight[:, None, None] * state
    first_leaf = lax.axis_index("scen") * leaves
    local_id = jnp.maximum(ancestor - first_leaf, 0)
    slot_ids = jnp.arange(leaves, dtype=jnp.int32)
    member = (local_id[:, None, :] == slot_ids[None, :, None]).astype(jnp.float32)
    seg_sums = jnp.einsum("tgl,ltn->tgn", member, weighted, precision=highest)
    seg_weights = jnp.einsum("tgl,l->tg", member, leaf_weight, precision=highest)
    last_pick = (slot_ids[None, :] == local_id[:, leaves - 1][:, None]).astype(jnp.float32)
    first_pick = (slot_ids[None, :] == 0).astype(jnp.float32)
    tail_sum = jnp.einsum("tg,tgn->tn", last_pick, seg_sums, precision=highest)
    tail_weight = jnp.sum(last_pick * seg_weights, axis=1)
    continued = (ancestor[:, 0] < first_leaf).astype(jnp.float32)
    spanning = (ancestor[:, leaves - 1] < first_leaf).astype(jnp.float32)
    head_sum = seg_sums[:, 0, :] * continued[:, None]
    head_weight = seg_weights[:, 0] * continued
    gathered = (
        lax.all_gather(tail_sum[None], "scen", axis=0, tiled=True),
        lax.all_gather(tail_weight[None], "scen", axis=0, tiled=True),
        lax.all_gather(head_sum[None], "scen", axis=0, tiled=True),
        lax.all_gather(head_weight[None], "scen", axis=0, tiled=True),
        lax.all_gather(spanning[None], "scen", axis=0, tiled=True),
    )
    position = lax.axis_index("scen")
    group_ids = jnp.arange(gathered[0].shape[0], dtype=jnp.int32)
    blank = (jnp.zeros_like(tail_sum), jnp.zeros_like(tail_weight), jnp.ones_like(spanning))

    def forward_step(carry, item):
        group, part_sum, part_weight, part_flag = item
        joined = link_terms(carry, (part_sum, part_weight, part_flag))
        keep = group < position
        return (
            jax.tree.map(lambda new_val, old_val: jnp.where(keep, new_val, old_val), joined, carry),
            None,
        )

    def backward_step(carry, item):
        group, part_sum, part_weight, part_flag = item
        joined = link_terms(carry, (part_sum, part_weight, part_flag))
        keep = group > position
        return (
            jax.tree.map(lambda new_val, old_val: jnp.where(keep, new_val, old_val), joined, carry),
            None,
        )

    before, unused = lax.scan(
        forward_step, blank, (group_ids, gathered[0], gathered[1], gathered[4])
    )
    after, unused = lax.scan(
        backward_step, blank, (group_ids, gathered[2], gathered[3], gathered[4]), reverse=True
    )
    open_front = first_pick * continued[:, None]
    seg_total = (
        seg_sums
        + open_front[:, :, None] * before[0][:, None, :]
        + last_pick[:, :, None] * after[0][:, None, :]
    )
    weight_total = seg_weights + open_front * before[1][:, None] + last_pick * after[1][:, None]
    leaf_sums = jnp.einsum("tgl,tgn->ltn", member, seg_total, precision=highest)
    leaf_weights = jnp.einsum("tgl,tg->lt", member, weight_total, precision=highest)
    average = leaf_sums / leaf_weights[:, :, None]
    new_dual = dual + penalty * (state - average)
    return (state, average, new_dual)


def solution(mesh):
    return jax.shard_map(
        local,
        mesh=mesh,
        in_specs=(
            P("scen", None, "feeder"),
            P("scen", None, "feeder"),
            P("scen", None, "feeder"),
            P("scen", None),
            P("scen"),
            P("feeder", None),
            P("feeder"),
            P("feeder", None, None),
            P(None, "scen"),
        ),
        out_specs=(P("scen", None, "feeder"), P("scen", None, "feeder"), P("scen", None, "feeder")),
        check_vma=False,
    )
```

profile of v0, /device:TPU:32, one launch (start us, length us, event | category | flops | bytes accessed | tf_op | source)
XLA Modules:
  0.0 681.2 jit_solution(15530600553333728089)
XLA Ops:
  0.6 0.7 convert_bitcast_fusion
  2.1 0.9 copy-done
  3.9 68.3 %psum.56 = f32[16,24]{1,0:T(8,128)S(1)} all-reduce(f32[16,24]{1,0:T(8,128)S(1)} %convert_reduce_fusion), channel_id=1, replica_groups=mesh['feeder'=32,'scen'=16] {'feeder'}, use_global_device_ids=true, to_apply=%region_1.0 | all-reduce | flops 384 | bytes 3072 | tf_op jit(solution)/shard_map/psum | solution.py:38
  72.2 1.4 fusion.74
  73.6 63.7 %psum.57 = f32[16,24]{1,0:T(8,128)S(1)} all-reduce(f32[16,24]{1,0:T(8,128)S(1)} %get-tuple-element.314), channel_id=1, replica_groups=mesh['feeder'=32,'scen'=16] {'feeder'}, use_global_device_ids=true, to_apply=%region_3.4 | all-reduce | flops 384 | bytes 3072 | tf_op jit(solution)/shard_map/psum | solution.py:38
  137.4 0.9 fusion.93
  138.2 63.7 %psum.58 = f32[16,24]{1,0:T(8,128)S(1)} all-reduce(f32[16,24]{1,0:T(8,128)S(1)} %get-tuple-element.320), channel_id=1, replica_groups=mesh['feeder'=32,'scen'=16] {'feeder'}, use_global_device_ids=true, to_apply=%region_5.6 | all-reduce | flops 384 | bytes 3072 | tf_op jit(solution)/shard_map/psum | solution.py:38
  202.5 63.7 %psum.59 = f32[16,24]{1,0:T(8,128)S(1)} all-reduce(f32[16,24]{1,0:T(8,128)S(1)} %get-tuple-element.322), channel_id=1, replica_groups=mesh['feeder'=32,'scen'=16] {'feeder'}, use_global_device_ids=true, to_apply=%region_7.8 | all-reduce | flops 384 | bytes 3072 | tf_op jit(solution)/shard_map/psum | solution.py:38
  266.8 63.7 %psum.60 = f32[16,24]{1,0:T(8,128)S(1)} all-reduce(f32[16,24]{1,0:T(8,128)S(1)} %get-tuple-element.324), channel_id=1, replica_groups=mesh['feeder'=32,'scen'=16] {'feeder'}, use_global_device_ids=true, to_apply=%region_9.10 | all-reduce | flops 384 | bytes 3072 | tf_op jit(solution)/shard_map/psum | solution.py:38
  331.1 63.7 %psum.61 = f32[16,24]{1,0:T(8,128)S(1)} all-reduce(f32[16,24]{1,0:T(8,128)S(1)} %get-tuple-element.326), channel_id=1, replica_groups=mesh['feeder'=32,'scen'=16] {'feeder'}, use_global_device_ids=true, to_apply=%region_11.12 | all-reduce | flops 384 | bytes 3072 | tf_op jit(solution)/shard_map/psum | solution.py:38
  394.8 1.4 fusion.97
  396.1 63.7 %psum.62 = f32[16,24]{1,0:T(8,128)S(1)} all-reduce(f32[16,24]{1,0:T(8,128)S(1)} %get-tuple-element.328), channel_id=1, replica_groups=mesh['feeder'=32,'scen'=16] {'feeder'}, use_global_device_ids=true, to_apply=%region_13.14 | all-reduce | flops 384 | bytes 3072 | tf_op jit(solution)/shard_map/psum | solution.py:38
  459.8 2.0 fusion.98
  461.8 63.7 %psum.63 = f32[16,24]{1,0:T(8,128)S(1)} all-reduce(f32[16,24]{1,0:T(8,128)S(1)} %get-tuple-element.330), channel_id=1, replica_groups=mesh['feeder'=32,'scen'=16] {'feeder'}, use_global_device_ids=true, to_apply=%region_15.16 | all-reduce | flops 384 | bytes 3072 | tf_op jit(solution)/shard_map/psum | solution.py:38
  526.2 1.4 broadcast_multiply_fusion
  527.5 0.7 copy-done.6
  528.3 1.0 fusion.48
  529.9 37.7 %all-gather = f32[384,512]{1,0:T(8,128)S(1)} all-gather(f32[24,512]{1,0:T(8,128)S(1)} %bitcast.122), channel_id=2, replica_groups=mesh['feeder'=32,'scen'=16] {'scen'}, dimensions={0}, use_global_device_ids=true | all-gather | bytes 835584 | tf_op jit(solution)/shard_map/all_gather | solution.py:59
  568.0 1.3 dynamic-slice
  570.3 30.1 %all-reduce.3 = (f32[384]{0:T(512)S(1)}, f32[384]{0:T(512)S(1)}, f32[384]{0:T(512)S(1)}) all-reduce(f32[384]{0:T(512)S(1)} %fusion.86, f32[384]{0:T(512)S(1)} %fusion.84, f32[384]{0:T(512)S(1)} %dynamic-update-slice.1), channel_id=3, replica_groups=mesh['feeder'=32,'scen'=16] {'scen'}, use_global_device_ids=true, to_apply=%add | all-reduce | flops 1152 | bytes 9216
  600.6 23.5 %while.30 = (s32[]{:T(128)}, f32[24,512]{1,0:T(8,128)S(1)}, f32[24]{0:T(128)S(1)}, s32[16]{0:T(128)S(1)}, s32[]{:T(128)}, /*index=5*/f32[16,24,512]{2,1,0:T(8,12...) while((s32[]{:T(128)}, f32[24,512]{1,0:T(8,128)S(1)}, ...), condition=%wide.region_18.19_spmd.clone, body=%wide.region_17.18_spmd.clone.sunk | while | flops 49252 | bytes 148175 | solution.py:87
  600.6 0.7 dynamic_slice.91
  602.1 0.7 dynamic_slice.91
  603.5 0.7 dynamic_slice.91
  605.0 0.7 dynamic_slice.91
  606.5 0.7 dynamic_slice.91
  607.9 0.7 dynamic_slice.91
  609.4 0.7 dynamic_slice.91
  610.9 0.7 dynamic_slice.91
  612.3 0.7 dynamic_slice.91
  613.8 0.7 dynamic_slice.91
  615.3 0.7 dynamic_slice.91
  616.7 0.7 dynamic_slice.91
  618.2 0.7 dynamic_slice.91
  619.7 0.7 dynamic_slice.91
  621.1 0.7 dynamic_slice.91
  624.2 30.1 %all_gather.18 = f32[16,24,512]{2,1,0:T(8,128)S(1)} all-gather(f32[1,24,512]{2,1,0:T(8,128)S(1)} %copy.24), channel_id=1, replica_groups=mesh['feeder'=32,'scen'=16] {'scen'}, dimensions={0}, use_global_device_ids=true | all-gather | bytes 835584 | tf_op jit(solution)/shard_map/all_gather | solution.py:61
  654.4 23.5 %while.31 = (s32[]{:T(128)}, f32[24,512]{1,0:T(8,128)S(1)}, f32[24]{0:T(128)S(1)}, s32[16]{0:T(128)S(1)}, s32[]{:T(128)}, /*index=5*/f32[16,24,512]{2,1,0:T(8,12...) while((s32[]{:T(128)}, f32[24,512]{1,0:T(8,128)S(1)}, ...), condition=%wide.region_20.21_spmd.clone, body=%wide.region_19.20_spmd.clone.sunk | while | flops 49253 | bytes 148195 | solution.py:90
  654.4 0.7 dynamic_slice.94
  655.9 0.7 dynamic_slice.94
  657.4 0.7 dynamic_slice.94
  670.6 0.7 dynamic_slice.94
  672.1 0.7 dynamic_slice.94
  673.5 0.7 dynamic_slice.94
  675.0 0.7 dynamic_slice.94
  676.5 0.7 dynamic_slice.94
  678.2 0.7 fusion.50
  679.5 1.7 subtract_add_fusion
  (141 shorter events, 15.7 us)
Async XLA Ops:
  0.6 1.4 copy-start.4
  2.0 1.0 copy-start
  3.0 0.7 copy-start.7
  3.0 69.2 %copy-start.2 = (f32[16,24,512]{2,1,0:T(8,128)S(1)}, f32[16,24,512]{2,1,0:T(8,128)}, u32[]{:S(2)}) copy-start(f32[16,24,512]{2,1,0:T(8,128)} %param.15) | copy-start | bytes 2359300
  3.8 68.4 %copy-start.5 = (f32[16,24]{1,0:T(8,128)S(1)}, f32[16,24]{1,0:T(8,128)}, u32[]{:S(2)}) copy-start(f32[16,24]{1,0:T(8,128)} %param.16) | copy-start | bytes 4612
  525.5 0.7 copy-start.8
  527.5 0.7 copy-start.6
  678.2 1.1 copy-start.1
  678.2 1.4 copy-start.3
where the time goes:
time: 682 us; the launch traced here: 681 us
  blocking collectives  612 us (90%)
  local copies, waits for them, and re-layouts  27 us (4%)
  loops' own time  22.6 us (3%)
  matrix products  10.1 us (1%)
  other arithmetic  7.87 us (1%)
    psum x8, blocking collectives, local(): head = lax.psum(jnp.sum(state, axis=2), 'feeder') / total_nodes  514 us
    all_gather x1, blocking collectives, local(): lax.all_gather(tail_sum[None], 'scen', axis=0, tiled=True)  37.7 us
    all_gather x1, blocking collectives, local(): lax.all_gather(head_sum[None], 'scen', axis=0, tiled=True)  30.1 us
    unnamed x1, blocking collectives  30.1 us
    dynamic_slice x32, local copies, waits for them, and re-layouts, local(): lax.scan(forward_step, blank, (group_ids, gathered[0], gathered[1], gathe...  21.2 us

commit v1 on v0

--- a/solution.py
+++ b/solution.py
@@ -8,6 +8,13 @@
 step_size = 0.08
 coupling = 4.0
 power_limit = 2.0
+
+
+def all_by_exchange(shard, name, dim):
+    size = lax.axis_size(name)
+    shards = jnp.stack([shard for _ in range(size)])
+    shards = lax.all_to_all(shards, name, split_axis=0, concat_axis=0)
+    return jnp.concatenate(shards, axis=dim)
 
 
 def link_terms(earlier, later):
@@ -58,7 +65,7 @@
     gathered = (
         lax.all_gather(tail_sum[None], "scen", axis=0, tiled=True),
         lax.all_gather(tail_weight[None], "scen", axis=0, tiled=True),
-        lax.all_gather(head_sum[None], "scen", axis=0, tiled=True),
+        all_by_exchange(head_sum[None], "scen", 0),
         lax.all_gather(head_weight[None], "scen", axis=0, tiled=True),
         lax.all_gather(spanning[None], "scen", axis=0, tiled=True),
     )

time: 682 us -> 704 us (1.032)
  starting transfers between devices: 0 us -> 15.1 us
  other arithmetic: 7.87 us -> 22.9 us
    all_gather x1 -> x0, blocking collectives: 30.1 us -> none  [local(): lax.all_gather(head_sum[None], 'scen', axis=0, tiled=True)]
    all_gather x1, blocking collectives: 37.7 us -> 64.3 us  [local(): lax.all_gather(tail_sum[None], 'scen', axis=0, tiled=True)]
    all_to_all x0 -> x1, starting transfers between devices: none -> 15.1 us  [all_by_exchange(): shards = lax.all_to_all(shards, name, split_axis=0, concat_axis=0)]
    select_n x32, other arithmetic: 1.58 us -> 14.4 us  [forward_step(): jnp.where(keep, new_val, old_val)]
  transfers between devices with their start and end apart: 0 -> 1, of which waited for: 0 -> 0; matrix products, arithmetic and copies ran while one was open for 0% -> 4% of each run, Pallas kernels for 0% -> 0%
where the time goes in v1:
time: 704 us; the launch traced here: 702 us
  blocking collectives  608 us (86%)
  local copies, waits for them, and re-layouts  26.5 us (4%)
  other arithmetic  22.9 us (3%)
  loops' own time  20.9 us (3%)
  starting transfers between devices  15.1 us (2%)
    psum x8, blocking collectives, local(): head = lax.psum(jnp.sum(state, axis=2), 'feeder') / total_nodes  514 us
    all_gather x1, blocking collectives, local(): lax.all_gather(tail_sum[None], 'scen', axis=0, tiled=True)  64.3 us
    unnamed x1, blocking collectives  29.3 us
    dynamic_slice x32, local copies, waits for them, and re-layouts, local(): lax.scan(forward_step, blank, (group_ids, gathered[0], gathered[1], gathe...  19.7 us
    all_to_all x1, starting transfers between devices, all_by_exchange(): shards = lax.all_to_all(shards, name, split_axis=0, concat_axis=0)  15.1 us
    select_n x32, other arithmetic, forward_step(): jnp.where(keep, new_val, old_val)  14.4 us
  transfers between devices with their start and end apart: 1, of which 0 were waited for; matrix products, arithmetic and copies ran while one was open for 4% of the time, Pallas kernels for 0%

profile of v1, /device:TPU:32, one launch (start us, length us, event | category | flops | bytes accessed | tf_op | source)
XLA Modules:
  0.0 702.0 jit_solution(9320012420796091418)
XLA Ops:
  0.6 0.7 subtract_maximum_fusion
  1.4 0.7 fusion.81
  2.1 1.2 convert_reduce_fusion
  3.3 68.3 %psum.56 = f32[16,24]{1,0:T(8,128)S(1)} all-reduce(f32[16,24]{1,0:T(8,128)S(1)} %convert_reduce_fusion), channel_id=1, replica_groups=mesh['feeder'=32,'scen'=16] {'feeder'}, use_global_device_ids=true, to_apply=%region_1.0 | all-reduce | flops 384 | bytes 3072 | tf_op jit(solution)/shard_map/psum | solution.py:45
  72.4 0.9 copy-done
  75.0 63.7 %psum.57 = f32[16,24]{1,0:T(8,128)S(1)} all-reduce(f32[16,24]{1,0:T(8,128)S(1)} %get-tuple-element.306), channel_id=1, replica_groups=mesh['feeder'=32,'scen'=16] {'feeder'}, use_global_device_ids=true, to_apply=%region_3.4 | all-reduce | flops 384 | bytes 3072 | tf_op jit(solution)/shard_map/psum | solution.py:45
  138.7 0.9 fusion.92
  139.5 63.7 %psum.58 = f32[16,24]{1,0:T(8,128)S(1)} all-reduce(f32[16,24]{1,0:T(8,128)S(1)} %get-tuple-element.312), channel_id=1, replica_groups=mesh['feeder'=32,'scen'=16] {'feeder'}, use_global_device_ids=true, to_apply=%region_5.6 | all-reduce | flops 384 | bytes 3072 | tf_op jit(solution)/shard_map/psum | solution.py:45
  203.8 63.7 %psum.59 = f32[16,24]{1,0:T(8,128)S(1)} all-reduce(f32[16,24]{1,0:T(8,128)S(1)} %get-tuple-element.314), channel_id=1, replica_groups=mesh['feeder'=32,'scen'=16] {'feeder'}, use_global_device_ids=true, to_apply=%region_7.8 | all-reduce | flops 384 | bytes 3072 | tf_op jit(solution)/shard_map/psum | solution.py:45
  268.1 63.7 %psum.60 = f32[16,24]{1,0:T(8,128)S(1)} all-reduce(f32[16,24]{1,0:T(8,128)S(1)} %get-tuple-element.316), channel_id=1, replica_groups=mesh['feeder'=32,'scen'=16] {'feeder'}, use_global_device_ids=true, to_apply=%region_9.10 | all-reduce | flops 384 | bytes 3072 | tf_op jit(solution)/shard_map/psum | solution.py:45
  332.4 63.7 %psum.61 = f32[16,24]{1,0:T(8,128)S(1)} all-reduce(f32[16,24]{1,0:T(8,128)S(1)} %get-tuple-element.318), channel_id=1, replica_groups=mesh['feeder'=32,'scen'=16] {'feeder'}, use_global_device_ids=true, to_apply=%region_11.12 | all-reduce | flops 384 | bytes 3072 | tf_op jit(solution)/shard_map/psum | solution.py:45
  396.7 63.7 %psum.62 = f32[16,24]{1,0:T(8,128)S(1)} all-reduce(f32[16,24]{1,0:T(8,128)S(1)} %get-tuple-element.320), channel_id=1, replica_groups=mesh['feeder'=32,'scen'=16] {'feeder'}, use_global_device_ids=true, to_apply=%region_13.14 | all-reduce | flops 384 | bytes 3072 | tf_op jit(solution)/shard_map/psum | solution.py:45
  461.0 63.7 %psum.63 = f32[16,24]{1,0:T(8,128)S(1)} all-reduce(f32[16,24]{1,0:T(8,128)S(1)} %get-tuple-element.322), channel_id=1, replica_groups=mesh['feeder'=32,'scen'=16] {'feeder'}, use_global_device_ids=true, to_apply=%region_15.16 | all-reduce | flops 384 | bytes 3072 | tf_op jit(solution)/shard_map/psum | solution.py:45
  524.8 0.7 copy-done.9
  525.9 1.0 fusion.48
  527.1 1.0 stack.3
  528.1 15.1 %all-to-all-start = ((f32[16,1,24,512]{3,2,1,0:T(8,128)}), f32[16,1,24,512]{3,2,1,0:T(8,128)S(1)}, u32[]{:S(2)}, u32[]{:S(2)}) async-start(f32[16,1,24,512]{3,2,1,0:T(8,128)} %stack.3), calls=%async_computation | async-start | bytes 1572864 | tf_op jit(solution)/shard_map/all_to_all | solution.py:16
  544.0 64.3 %all-gather = f32[384,512]{1,0:T(8,128)} all-gather(f32[24,512]{1,0:T(8,128)S(1)} %bitcast.122), channel_id=2, replica_groups=mesh['feeder'=32,'scen'=16] {'scen'}, dimensions={0}, use_global_device_ids=true | all-gather | bytes 835584 | tf_op jit(solution)/shard_map/all_gather | solution.py:66
  608.5 1.3 dynamic-slice
  610.5 0.8 fusion.85
  611.4 0.8 fusion.83
  612.2 29.3 %all-reduce.3 = (f32[384]{0:T(512)S(1)}, f32[384]{0:T(512)S(1)}, f32[384]{0:T(512)S(1)}) all-reduce(f32[384]{0:T(512)S(1)} %fusion.85, f32[384]{0:T(512)S(1)} %fusion.83, f32[384]{0:T(512)S(1)} %dynamic-update-slice.1), channel_id=3, replica_groups=mesh['feeder'=32,'scen'=16] {'scen'}, use_global_device_ids=true, to_apply=%add | all-reduce | flops 1152 | bytes 9216
  641.7 35.1 %while.30 = (s32[]{:T(128)}, f32[24,512]{1,0:T(8,128)S(1)}, f32[24]{0:T(128)S(1)}, s32[16]{0:T(128)S(1)}, s32[]{:T(128)}, /*index=5*/f32[16,24,512]{2,1,0:T(8,12...) while((s32[]{:T(128)}, f32[24,512]{1,0:T(8,128)S(1)}, ...), condition=%wide.region_18.19_spmd.clone, body=%wide.region_17.18_spmd.clone.sunk | while | flops 49252 | bytes 148175 | solution.py:94
  641.7 0.7 dynamic_slice.91
  643.1 0.9 fusion.106
  643.9 0.6 dynamic_slice.91
  645.3 0.9 fusion.106
  646.1 0.6 dynamic_slice.91
  647.4 0.9 fusion.106
  648.3 0.6 dynamic_slice.91
  649.6 0.9 fusion.106
  650.5 0.6 dynamic_slice.91
  651.8 0.9 fusion.106
  652.7 0.6 dynamic_slice.91
  654.0 0.9 fusion.106
  656.2 0.9 fusion.106
  658.4 0.9 fusion.106
  660.6 0.9 fusion.106
  662.8 0.9 fusion.106
  665.0 0.9 fusion.106
  667.2 0.9 fusion.106
  669.4 0.9 fusion.106
  671.6 0.9 fusion.106
  673.7 0.9 fusion.106
  675.9 0.9 fusion.106
  677.0 21.5 %while.31 = (s32[]{:T(128)}, f32[24,512]{1,0:T(8,128)S(1)}, f32[24]{0:T(128)S(1)}, s32[16]{0:T(128)S(1)}, s32[]{:T(128)}, /*index=5*/f32[16,24,512]{2,1,0:T(8,12...) while((s32[]{:T(128)}, f32[24,512]{1,0:T(8,128)S(1)}, ...), condition=%wide.region_20.21_spmd.clone, body=%wide.region_19.20_spmd.clone.sunk | while | flops 49253 | bytes 148195 | solution.py:97
  699.0 0.7 fusion.50
  700.2 1.8 subtract_add_fusion
  (145 shorter events, 26.1 us)
Async XLA Ops:
  0.6 1.4 copy-start.7
  1.4 0.7 copy-start.8
  2.1 70.2 %copy-start.4 = (bf16[512,512]{1,0:T(8,128)(2,1)S(1)}, bf16[512,512]{1,0:T(8,128)(2,1)}, u32[]{:S(2)}) copy-start(bf16[512,512]{1,0:T(8,128)(2,1)} %param.18) | copy-start | bytes 1572868
  72.3 1.0 copy-start
  73.3 0.7 copy-start.5
  73.3 1.1 copy-start.2
  73.3 1.2 copy-start.6
  524.8 0.7 copy-start.9
  525.9 173.8 %copy-start.1 = (f32[16,24,512]{2,1,0:T(8,128)}, f32[16,24,512]{2,1,0:T(8,128)S(1)}, u32[]{:S(2)}) copy-start(f32[16,24,512]{2,1,0:T(8,128)S(1)} %get-tuple-element.325) | copy-start | bytes 2359300
  528.1 148.9 %all-to-all-start = ((f32[16,1,24,512]{3,2,1,0:T(8,128)}), f32[16,1,24,512]{3,2,1,0:T(8,128)S(1)}, u32[]{:S(2)}, u32[]{:S(2)}) async-start(f32[16,1,24,512]{3,2,1,0:T(8,128)} %stack.3), calls=%async_computation | async-start | bytes 1572864 | tf_op jit(solution)/shard_map/all_to_all | solution.py:16
  699.0 1.1 copy-start.3
